TPU v7x, 512 devices: a whole 4x8x8 slice. The times are simulated.
512 devices in a mesh: segment: 4 (over x), chan: 16 (over y, core), dp: 8 (over z).
Axes of the slice: x: 4, y: 8, z: 8, core: 2. Of those that a mesh axis runs over, the one named last changes fastest.
Arguments:
- grad_top: bfloat16 [8, 1536, 256], P('dp', None, 'chan'), may hold values from -6 to 6
- inputs_one: bfloat16 [4, 8, 1536, 256], P('segment', 'dp', 'chan'), may hold values from -6 to 6
- conv_one: bfloat16 [4, 8, 1536, 256], P('segment', 'dp', 'chan'), may hold values from -130 to 130
- inputs_two: bfloat16 [4, 8, 1536, 256], P('segment', 'dp', 'chan'), may hold values from -6 to 6
- conv_two: bfloat16 [4, 8, 1536, 256], P('segment', 'dp', 'chan'), may hold values from -130 to 130
- proj_weight: bfloat16 [4, 2, 1536, 1536], P('segment', None, 'chan'), may hold values from -0.15625 to 0.15625
- conv_weight: bfloat16 [4, 2, 1536, 432], P('segment', None, 'chan'), may hold values from -0.3125 to 0.3125
- norm_gain: float32 [4, 2, 1536], P('segment', None, 'chan'), may hold values from 0.1 to 1.9
- norm_bias: float32 [4, 2, 1536], P('segment', None, 'chan'), may hold values from -4 to 4
Outputs:
- grad_latent: bfloat16 [4, 8, 1536, 256], P('segment', 'dp', None, 'chan')
- grad_proj: float32 [4, 2, 1536, 1536], P('segment', None, 'chan')
- grad_conv: float32 [4, 2, 1536, 432], P('segment', None, 'chan')
- grad_gain: float32 [4, 2, 1536], P('segment', None, 'chan')
- grad_bias: float32 [4, 2, 1536], P('segment', None, 'chan')
All inputs are finite; a program needn't handle non-finite values.
Results may differ from a plain program's by a relative error of at most 0.009.
Values may be sent and summed in bfloat16 or wider, within the bound.
No kernel may reach another device: no remote copies, remote signals or barrier semaphores. Data moves between devices by JAX's collectives and lax.ppermute only.
A program may use at most 64 MiB of HBM per device.

v0:
```python
import jax
import jax.numpy as jnp
from jax import lax
from jax.sharding import PartitionSpec as P

GS = 48
WW = 64
NORM_EPS = 1e-05


def passed_along(block, axis, distance):
    devices = range(lax.axis_size(axis))
    route = [(i - distance, i) for i in devices if i - distance in devices]
    return lax.ppermute(block, axis, route)


def shifted_cells(values, step_row, step_col, img_width):
    length = values.shape[2]
    margin = img_width + 1
    padded = jnp.pad(values, ((0, 0), (0, 0), (margin, margin)))
    start_at = margin + step_row * img_width + step_col
    part_view = lax.slice_in_dim(padded, start_at, start_at + length, axis=2)
    column = jnp.arange(length, dtype=jnp.int32) % img_width
    inside = (column + step_col >= 0) & (column + step_col < img_width)
    return jnp.where(inside, part_view, jnp.zeros((), values.dtype))


def norm_forward(saved_pre, gain_vec, bias_vec):
    chans, positions = saved_pre.shape
    groups_here = chans // GS
    pre = saved_pre.astype(jnp.float32).reshape(groups_here, GS, positions)
    centre = jnp.mean(pre, axis=(1, 2), keepdims=True)
    varied = jnp.mean(jnp.square(pre - centre), axis=(1, 2), keepdims=True)
    inv_std = lax.rsqrt(varied + NORM_EPS)
    normed = (pre - centre) * inv_std
    gain_grid = gain_vec.reshape(groups_here, GS, 1)
    scaled = normed * gain_grid + bias_vec.reshape(groups_here, GS, 1)
    gate_vals = jax.nn.sigmoid(scaled)
    act_bf = (scaled * gate_vals).astype(jnp.bfloat16).reshape(chans, positions)
    return (normed, scaled, gate_vals, inv_std, gain_grid, act_bf)


def conv_backward(grad_act, norm_state, saved_in, w_conv):
    normed, scaled, gate_vals, inv_std, gain_grid, act_bf = norm_state
    groups_here, _, positions = normed.shape
    chans = groups_here * GS
    grad_act = grad_act.reshape(groups_here, GS, positions)
    grad_norm = grad_act * (gate_vals * (1.0 + scaled * (1.0 - gate_vals)))
    gain_grad = jnp.sum(grad_norm * normed, axis=2).reshape(chans)
    bias_grad = jnp.sum(grad_norm, axis=2).reshape(chans)
    weighted = grad_norm * gain_grid
    first_mean = jnp.mean(weighted, axis=(1, 2), keepdims=True)
    second_mean = jnp.mean(weighted * normed, axis=(1, 2), keepdims=True)
    grad_pre = (inv_std * (weighted - first_mean - normed * second_mean)).astype(jnp.bfloat16)
    saved_grid = saved_in.reshape(groups_here, GS, positions)
    taps_w = w_conv.reshape(groups_here, GS, 9, GS)
    conv_parts = []
    back_sum = jnp.zeros((groups_here, GS, positions), jnp.float32)
    for tap_row in (-1, 0, 1):
        for tap_col in (-1, 0, 1):
            tap_at = 3 * (tap_row + 1) + tap_col + 1
            source = shifted_cells(saved_grid, tap_row, tap_col, WW)
            conv_parts.append(
                jnp.einsum("gop,gjp->goj", grad_pre, source, preferred_element_type=jnp.float32)
            )
            spread_back = jnp.einsum(
                "goj,gop->gjp",
                taps_w[:, :, tap_at, :],
                grad_pre,
                preferred_element_type=jnp.float32,
            )
            back_sum = back_sum + shifted_cells(spread_back, -tap_row, -tap_col, WW)
    conv_grad = jnp.stack(conv_parts, axis=2).reshape(chans, 9 * GS)
    branch = back_sum.reshape(chans, positions).astype(jnp.bfloat16)
    return (branch, conv_grad, gain_grad, bias_grad)


def block_sharded(grad_slab, saved_in, saved_pre, w_proj, w_conv, gain_vec, bias_vec):
    norm_state = norm_forward(saved_pre, gain_vec, bias_vec)
    act_bf = norm_state[5]
    grad_piece = lax.all_gather(grad_slab, "chan", axis=1, tiled=True)
    fresh = jnp.dot(w_proj, grad_piece, preferred_element_type=jnp.float32)
    weight_acc = lax.dot_general(
        act_bf, grad_piece, (((1,), (1,)), ((), ())), preferred_element_type=jnp.float32
    )
    branch, conv_grad, gain_grad, bias_grad = conv_backward(fresh, norm_state, saved_in, w_conv)
    returned = lax.all_to_all(branch, "chan", split_axis=1, concat_axis=0, tiled=True)
    out_slab = (grad_slab.astype(jnp.float32) + returned.astype(jnp.float32)).astype(jnp.bfloat16)
    return (out_slab, (weight_acc, conv_grad, gain_grad, bias_grad))


def take_micro(saved_all, index_at):
    return lax.dynamic_index_in_dim(saved_all[0], index_at, 0, keepdims=False)


def per_device(
    grad_top,
    inputs_one,
    conv_one,
    inputs_two,
    conv_two,
    proj_weight,
    conv_weight,
    norm_gain,
    norm_bias,
):
    segments = lax.axis_size("segment")
    segment_at = lax.axis_index("segment")
    local_mb = grad_top.shape[0]
    chans = conv_one.shape[2]
    width_all = proj_weight.shape[3]
    ticks = local_mb + segments - 1
    initial = (
        jnp.zeros(grad_top.shape[1:], jnp.bfloat16),
        jnp.zeros((1,) + grad_top.shape, jnp.bfloat16),
        jnp.zeros((2, chans, width_all), jnp.float32),
        jnp.zeros((2, chans, 9 * GS), jnp.float32),
        jnp.zeros((2, chans), jnp.float32),
        jnp.zeros((2, chans), jnp.float32),
    )

    def one_tick(tick_at, running):
        received, latent, proj_acc, conv_acc, gain_acc, bias_acc = running
        micro_at = tick_at - (segments - 1 - segment_at)
        is_valid = (micro_at >= 0) & (micro_at < local_mb)
        safe_mb = jnp.clip(micro_at, 0, local_mb - 1)
        top_grad = lax.dynamic_index_in_dim(grad_top, safe_mb, 0, keepdims=False)
        entering = jnp.where(segment_at == segments - 1, top_grad, received)
        mid_grad, grads_two = block_sharded(
            entering,
            take_micro(inputs_two, safe_mb),
            take_micro(conv_two, safe_mb),
            proj_weight[0, 1],
            conv_weight[0, 1],
            norm_gain[0, 1],
            norm_bias[0, 1],
        )
        out_grad, grads_one = block_sharded(
            mid_grad,
            take_micro(inputs_one, safe_mb),
            take_micro(conv_one, safe_mb),
            proj_weight[0, 0],
            conv_weight[0, 0],
            norm_gain[0, 0],
            norm_bias[0, 0],
        )
        weight_mask = is_valid.astype(jnp.float32)
        proj_acc = proj_acc + weight_mask * jnp.stack((grads_one[0], grads_two[0]))
        conv_acc = conv_acc + weight_mask * jnp.stack((grads_one[1], grads_two[1]))
        gain_acc = gain_acc + weight_mask * jnp.stack((grads_one[2], grads_two[2]))
        bias_acc = bias_acc + weight_mask * jnp.stack((grads_one[3], grads_two[3]))
        current = lax.dynamic_index_in_dim(latent[0], safe_mb, 0, keepdims=False)
        kept = jnp.where(is_valid, out_grad, current)
        latent = lax.dynamic_update_index_in_dim(latent, kept[None, None], safe_mb, 1)
        received = passed_along(out_grad, "segment", -1)
        return (received, latent, proj_acc, conv_acc, gain_acc, bias_acc)

    final = lax.fori_loop(0, ticks, one_tick, initial)
    latent = final[1]
    proj_sum, conv_sum, gain_sum, bias_sum = lax.psum(
        (final[2], final[3], final[4], final[5]), "dp"
    )
    return (latent, proj_sum[None], conv_sum[None], gain_sum[None], bias_sum[None])


def solution(mesh):
    return jax.shard_map(
        per_device,
        mesh=mesh,
        in_specs=(
            P("dp", None, "chan"),
            P("segment", "dp", "chan", None),
            P("segment", "dp", "chan", None),
            P("segment", "dp", "chan", None),
            P("segment", "dp", "chan", None),
            P("segment", None, "chan", None),
            P("segment", None, "chan", None),
            P("segment", None, "chan"),
            P("segment", None, "chan"),
        ),
        out_specs=(
            P("segment", "dp", None, "chan"),
            P("segment", None, "chan", None),
            P("segment", None, "chan", None),
            P("segment", None, "chan"),
            P("segment", None, "chan"),
        ),
        check_vma=False,
    )
```

profile of v0, /device:TPU:2, one launch (start us, length us, event | category | flops | bytes accessed | tf_op | source)
XLA Modules:
  0.0 469.4 jit_solution(2428649469921807830)
XLA Ops:
  7.3 1.8 copy.64
  9.6 357.8 %while.26 = (s32[]{:T(128)}, bf16[1536,16]{0,1:T(8,128)(2,1)S(1)}, bf16[1,1,1536,16]{2,3,1,0:T(8,128)(2,1)}, f32[2,96,1536]{2,1,0:T(8,128)S(1)}, f32[2,96,432]{1...) while((s32[]{:T(128)}, bf16[1536,16]{0,1:T(8,128)(2,1)S(1)}, ...), condition=%wide.region_21.22_spmd.clone, body=%wide.region_0.21_spmd.clone.sunk | while | flops 392720768 | bytes 27672152 | solution.py:158
  14.7 19.7 %all_gather.24 = bf16[1536,256]{0,1:T(8,128)(2,1)S(1)} all-gather(bf16[1536,16]{0,1:T(8,128)(2,1)S(1)} %bitcast_select_fusion.3), channel_id=1, replica_groups=mesh['segment'=4,'chan'=16,'dp'=8] {'chan'}, dimensions={1}, use_global_device_ids=true | all-gather | bytes 835584 | tf_op jit(solution)/shard_map/while/body/eval_jaxpr/all_gather | solution.py:81
  34.4 2.0 multiply_reduce_fusion.14
  40.7 4.4 all-to-all-start
  53.2 18.4 %all_gather.25 = bf16[1536,256]{0,1:T(8,128)(2,1)S(1)} all-gather(bf16[1536,16]{0,1:T(8,128)(2,1)S(1)} %add_convert_fusion.4), channel_id=1, replica_groups=mesh['segment'=4,'chan'=16,'dp'=8] {'chan'}, dimensions={1}, use_global_device_ids=true | all-gather | bytes 835584 | tf_op jit(solution)/shard_map/while/body/eval_jaxpr/all_gather | solution.py:81
  71.6 2.0 multiply_reduce_fusion.15
  76.8 4.6 all-to-all-start.1
  88.9 1.2 copy.167
  91.7 1.4 fusion.358
  93.2 3.9 collective-permute-start
  97.2 1.9 collective-permute-done
  104.2 19.4 %all_gather.24 = bf16[1536,256]{0,1:T(8,128)(2,1)S(1)} all-gather(bf16[1536,16]{0,1:T(8,128)(2,1)S(1)} %bitcast_select_fusion.3), channel_id=1, replica_groups=mesh['segment'=4,'chan'=16,'dp'=8] {'chan'}, dimensions={1}, use_global_device_ids=true | all-gather | bytes 835584 | tf_op jit(solution)/shard_map/while/body/eval_jaxpr/all_gather | solution.py:81
  123.6 2.0 multiply_reduce_fusion.14
  129.9 4.6 all-to-all-start
  141.4 1.0 all-to-all-done
  142.6 18.4 %all_gather.25 = bf16[1536,256]{0,1:T(8,128)(2,1)S(1)} all-gather(bf16[1536,16]{0,1:T(8,128)(2,1)S(1)} %add_convert_fusion.4), channel_id=1, replica_groups=mesh['segment'=4,'chan'=16,'dp'=8] {'chan'}, dimensions={1}, use_global_device_ids=true | all-gather | bytes 835584 | tf_op jit(solution)/shard_map/while/body/eval_jaxpr/all_gather | solution.py:81
  161.0 2.0 multiply_reduce_fusion.15
  166.3 4.6 all-to-all-start.1
  178.3 1.2 copy.167
  181.2 1.4 fusion.358
  182.6 3.9 collective-permute-start
  186.6 1.9 collective-permute-done
  193.7 19.4 %all_gather.24 = bf16[1536,256]{0,1:T(8,128)(2,1)S(1)} all-gather(bf16[1536,16]{0,1:T(8,128)(2,1)S(1)} %bitcast_select_fusion.3), channel_id=1, replica_groups=mesh['segment'=4,'chan'=16,'dp'=8] {'chan'}, dimensions={1}, use_global_device_ids=true | all-gather | bytes 835584 | tf_op jit(solution)/shard_map/while/body/eval_jaxpr/all_gather | solution.py:81
  213.1 2.0 multiply_reduce_fusion.14
  219.4 4.6 all-to-all-start
  230.9 1.0 all-to-all-done
  232.1 18.4 %all_gather.25 = bf16[1536,256]{0,1:T(8,128)(2,1)S(1)} all-gather(bf16[1536,16]{0,1:T(8,128)(2,1)S(1)} %add_convert_fusion.4), channel_id=1, replica_groups=mesh['segment'=4,'chan'=16,'dp'=8] {'chan'}, dimensions={1}, use_global_device_ids=true | all-gather | bytes 835584 | tf_op jit(solution)/shard_map/while/body/eval_jaxpr/all_gather | solution.py:81
  250.5 2.0 multiply_reduce_fusion.15
  255.7 4.6 all-to-all-start.1
  267.8 1.2 copy.167
  270.6 1.4 fusion.358
  272.1 3.9 collective-permute-start
  276.1 1.9 collective-permute-done
  283.1 19.4 %all_gather.24 = bf16[1536,256]{0,1:T(8,128)(2,1)S(1)} all-gather(bf16[1536,16]{0,1:T(8,128)(2,1)S(1)} %bitcast_select_fusion.3), channel_id=1, replica_groups=mesh['segment'=4,'chan'=16,'dp'=8] {'chan'}, dimensions={1}, use_global_device_ids=true | all-gather | bytes 835584 | tf_op jit(solution)/shard_map/while/body/eval_jaxpr/all_gather | solution.py:81
  302.5 2.0 multiply_reduce_fusion.14
  308.8 4.6 all-to-all-start
  321.5 18.4 %all_gather.25 = bf16[1536,256]{0,1:T(8,128)(2,1)S(1)} all-gather(bf16[1536,16]{0,1:T(8,128)(2,1)S(1)} %add_convert_fusion.4), channel_id=1, replica_groups=mesh['segment'=4,'chan'=16,'dp'=8] {'chan'}, dimensions={1}, use_global_device_ids=true | all-gather | bytes 835584 | tf_op jit(solution)/shard_map/while/body/eval_jaxpr/all_gather | solution.py:81
  339.9 2.0 multiply_reduce_fusion.15
  345.1 4.6 all-to-all-start.1
  357.2 1.2 copy.167
  360.0 1.4 fusion.358
  361.5 3.9 collective-permute-start
  365.5 1.9 collective-permute-done
  367.5 2.4 copy.65
  369.9 23.8 %all-reduce.18 = (f32[1,2,96]{2,1,0:T(2,128)}, f32[1,2,96]{2,1,0:T(2,128)}) all-reduce(f32[1,2,96]{2,1,0:T(2,128)S(1)} %bitcast.586, f32[1,2,96]{2,1,0:T(2,128)S(1)} %bitcast.587), channel_id=1, replica_groups=mesh['segment'=4,'chan'=16,'dp'=8] {'dp'}, use_global_device_ids=true, to_apply=%region_24.25 | all-reduce | flops 384 | bytes 3072 | tf_op jit(solution)/shard_map/psum | solution.py:160
  393.7 65.7 %all-reduce.22.cloned.1.call-done = (f32[1,2,96,1536]{3,2,1,0:T(8,128)}, f32[1,2,96,432]{3,2,1,0:T(8,128)}) async-done(((f32[1,2,96,1536]{3,2,1,0:T(8,128)}, f32[1,2,96,432]{3,2,1,0:T(8,128)}), (f32[1,2,96,1536]{3,2,1,0:T(8,128)}, f32[1,2,96,432]{3,2,1,0:T(8,128)})) %all-reduce.22.cloned.1.call-update) | async-done | bytes 1511440 | tf_op jit(solution)/shard_map/psum | solution.py:160
  459.4 2.4 copy.207
  (683 shorter events, 116.1 us)
Async XLA Ops:
  7.2 452.2 %all-reduce.22.cloned.1.call-start = ((), (), s32[]{:S(2)}) async-start(), calls=%async_computation.2 | async-start | bytes 3145728 | tf_op jit(solution)/shard_map/psum | solution.py:160
  9.7 29.8 %copy-start.30 = (pred[256]{0:T(512)(128)(4,1)}, pred[256]{0:T(512)(128)(4,1)S(1)}, u32[]{:S(2)}) copy-start(pred[256]{0:T(512)(128)(4,1)S(1)} %compare_and_fusion.7) | copy-start | bytes 772 | tf_op jit(solution)/shard_map/while
  9.7 29.8 %copy-start.27 = (pred[256]{0:T(512)(128)(4,1)}, pred[256]{0:T(512)(128)(4,1)S(1)}, u32[]{:S(2)}) copy-start(pred[256]{0:T(512)(128)(4,1)S(1)} %compare_and_fusion.8) | copy-start | bytes 772 | tf_op jit(solution)/shard_map/while
  39.5 9.8 %copy-start.7 = (bf16[1,1,96,256]{3,2,1,0:T(8,128)(2,1)S(1)}, bf16[1,1,96,256]{3,2,1,0:T(8,128)(2,1)}, u32[]{:S(2)}) copy-start(bf16[1,1,96,256]{3,2,1,0:T(8,128)(2,1)} %get-tuple-element.857) | copy-start | bytes 147460 | tf_op jit(solution)/shard_map/while
  39.8 9.5 %copy-start.31 = (pred[256]{0:T(512)(128)(4,1)S(1)}, pred[256]{0:T(512)(128)(4,1)}, u32[]{:S(2)}) copy-start(pred[256]{0:T(512)(128)(4,1)} %copy-done.30) | copy-start | bytes 772 | tf_op jit(solution)/shard_map/while
  39.8 9.9 %copy-start.28 = (pred[256]{0:T(512)(128)(4,1)S(1)}, pred[256]{0:T(512)(128)(4,1)}, u32[]{:S(2)}) copy-start(pred[256]{0:T(512)(128)(4,1)} %copy-done.27) | copy-start | bytes 772 | tf_op jit(solution)/shard_map/while
  40.7 12.3 %all-to-all-start = ((bf16[96,16,16]{0,2,1:T(8,128)(2,1)}), bf16[96,16,16]{0,2,1:T(8,128)(2,1)S(1)}, u32[]{:S(2)}, u32[]{:S(2)}) async-start(bf16[96,16,16]{0,2,1:T(8,128)(2,1)} %convert_element_type.430), calls=%async_computation | async-start | bytes 131072 | tf_op jit(solution)/shard_map/while/body/eval_jaxpr/all_to_all | solution.py:87
  52.0 19.6 %copy-start.22 = (f32[96]{0:T(128)S(1)}, f32[96]{0:T(128)}, u32[]{:S(2)}) copy-start(f32[96]{0:T(128)} %mul.953) | copy-start | bytes 1156 | tf_op jit(solution)/shard_map/while
  75.0 6.5 %copy-start.6 = (bf16[1,1,96,256]{3,2,1,0:T(8,128)(2,1)S(1)}, bf16[1,1,96,256]{3,2,1,0:T(8,128)(2,1)}, u32[]{:S(2)}) copy-start(bf16[1,1,96,256]{3,2,1,0:T(8,128)(2,1)} %get-tuple-element.856) | copy-start | bytes 147460 | tf_op jit(solution)/shard_map/while
  76.8 14.7 %all-to-all-start.1 = ((bf16[96,16,16]{0,2,1:T(8,128)(2,1)}), bf16[96,16,16]{0,2,1:T(8,128)(2,1)S(1)}, u32[]{:S(2)}, u32[]{:S(2)}) async-start(bf16[96,16,16]{0,2,1:T(8,128)(2,1)} %convert_element_type.431), calls=%async_computation.1 | async-start | bytes 131072 | tf_op jit(solution)/shard_map/while/body/eval_jaxpr/all_to_all | solution.py:87
  91.5 7.6 %copy-start.4 = (f32[2,96,432]{1,2,0:T(8,128)}, f32[2,96,432]{1,2,0:T(8,128)S(1)}, u32[]{:S(2)}) copy-start(f32[2,96,432]{1,2,0:T(8,128)S(1)} %fusion.378) | copy-start | bytes 995332 | tf_op jit(solution)/shard_map/while
  93.2 6.0 %collective-permute-start = (bf16[1536,16]{0,1:T(8,128)(2,1)S(1)}, bf16[1536,16]{0,1:T(8,128)(2,1)S(1)}, u32[]{:S(2)}, u32[]{:S(2)}) collective-permute-start(bf16[1536,16]{0,1:T(8,128)(2,1)S(1)} %get-tuple-element.790), channel_id=1, source_target_pairs={{128,0},{256,128},{384,256},{129,1},{257,129},{385,257},{130,2},{2... | collective-permute-start | bytes 147464 | tf_op jit(solution)/shard_map/while/body/eval_jaxpr/ppermute | solution.py:14
  99.2 29.5 %copy-start.30 = (pred[256]{0:T(512)(128)(4,1)}, pred[256]{0:T(512)(128)(4,1)S(1)}, u32[]{:S(2)}) copy-start(pred[256]{0:T(512)(128)(4,1)S(1)} %compare_and_fusion.7) | copy-start | bytes 772 | tf_op jit(solution)/shard_map/while
  99.2 29.5 %copy-start.27 = (pred[256]{0:T(512)(128)(4,1)}, pred[256]{0:T(512)(128)(4,1)S(1)}, u32[]{:S(2)}) copy-start(pred[256]{0:T(512)(128)(4,1)S(1)} %compare_and_fusion.8) | copy-start | bytes 772 | tf_op jit(solution)/shard_map/while
  128.0 6.5 %copy-start.2 = (bf16[1,1,96,256]{3,2,1,0:T(8,128)(2,1)S(1)}, bf16[1,1,96,256]{3,2,1,0:T(8,128)(2,1)}, u32[]{:S(2)}) copy-start(bf16[1,1,96,256]{3,2,1,0:T(8,128)(2,1)} %get-tuple-element.854) | copy-start | bytes 147460 | tf_op jit(solution)/shard_map/while
  128.7 10.0 %copy-start.7 = (bf16[1,1,96,256]{3,2,1,0:T(8,128)(2,1)S(1)}, bf16[1,1,96,256]{3,2,1,0:T(8,128)(2,1)}, u32[]{:S(2)}) copy-start(bf16[1,1,96,256]{3,2,1,0:T(8,128)(2,1)} %get-tuple-element.857) | copy-start | bytes 147460 | tf_op jit(solution)/shard_map/while
  129.0 9.7 %copy-start.31 = (pred[256]{0:T(512)(128)(4,1)S(1)}, pred[256]{0:T(512)(128)(4,1)}, u32[]{:S(2)}) copy-start(pred[256]{0:T(512)(128)(4,1)} %copy-done.30) | copy-start | bytes 772 | tf_op jit(solution)/shard_map/while
  129.0 10.1 %copy-start.28 = (pred[256]{0:T(512)(128)(4,1)S(1)}, pred[256]{0:T(512)(128)(4,1)}, u32[]{:S(2)}) copy-start(pred[256]{0:T(512)(128)(4,1)} %copy-done.27) | copy-start | bytes 772 | tf_op jit(solution)/shard_map/while
  129.9 12.5 %all-to-all-start = ((bf16[96,16,16]{0,2,1:T(8,128)(2,1)}), bf16[96,16,16]{0,2,1:T(8,128)(2,1)S(1)}, u32[]{:S(2)}, u32[]{:S(2)}) async-start(bf16[96,16,16]{0,2,1:T(8,128)(2,1)} %convert_element_type.430), calls=%async_computation | async-start | bytes 131072 | tf_op jit(solution)/shard_map/while/body/eval_jaxpr/all_to_all | solution.py:87
  141.4 19.6 %copy-start.22 = (f32[96]{0:T(128)S(1)}, f32[96]{0:T(128)}, u32[]{:S(2)}) copy-start(f32[96]{0:T(128)} %mul.953) | copy-start | bytes 1156 | tf_op jit(solution)/shard_map/while
  164.4 6.5 %copy-start.6 = (bf16[1,1,96,256]{3,2,1,0:T(8,128)(2,1)S(1)}, bf16[1,1,96,256]{3,2,1,0:T(8,128)(2,1)}, u32[]{:S(2)}) copy-start(bf16[1,1,96,256]{3,2,1,0:T(8,128)(2,1)} %get-tuple-element.856) | copy-start | bytes 147460 | tf_op jit(solution)/shard_map/while
  166.3 14.7 %all-to-all-start.1 = ((bf16[96,16,16]{0,2,1:T(8,128)(2,1)}), bf16[96,16,16]{0,2,1:T(8,128)(2,1)S(1)}, u32[]{:S(2)}, u32[]{:S(2)}) async-start(bf16[96,16,16]{0,2,1:T(8,128)(2,1)} %convert_element_type.431), calls=%async_computation.1 | async-start | bytes 131072 | tf_op jit(solution)/shard_map/while/body/eval_jaxpr/all_to_all | solution.py:87
  181.0 7.6 %copy-start.4 = (f32[2,96,432]{1,2,0:T(8,128)}, f32[2,96,432]{1,2,0:T(8,128)S(1)}, u32[]{:S(2)}) copy-start(f32[2,96,432]{1,2,0:T(8,128)S(1)} %fusion.378) | copy-start | bytes 995332 | tf_op jit(solution)/shard_map/while
  182.6 6.0 %collective-permute-start = (bf16[1536,16]{0,1:T(8,128)(2,1)S(1)}, bf16[1536,16]{0,1:T(8,128)(2,1)S(1)}, u32[]{:S(2)}, u32[]{:S(2)}) collective-permute-start(bf16[1536,16]{0,1:T(8,128)(2,1)S(1)} %get-tuple-element.790), channel_id=1, source_target_pairs={{128,0},{256,128},{384,256},{129,1},{257,129},{385,257},{130,2},{2... | collective-permute-start | bytes 147464 | tf_op jit(solution)/shard_map/while/body/eval_jaxpr/ppermute | solution.py:14
  188.6 29.5 %copy-start.30 = (pred[256]{0:T(512)(128)(4,1)}, pred[256]{0:T(512)(128)(4,1)S(1)}, u32[]{:S(2)}) copy-start(pred[256]{0:T(512)(128)(4,1)S(1)} %compare_and_fusion.7) | copy-start | bytes 772 | tf_op jit(solution)/shard_map/while
  188.7 29.5 %copy-start.27 = (pred[256]{0:T(512)(128)(4,1)}, pred[256]{0:T(512)(128)(4,1)S(1)}, u32[]{:S(2)}) copy-start(pred[256]{0:T(512)(128)(4,1)S(1)} %compare_and_fusion.8) | copy-start | bytes 772 | tf_op jit(solution)/shard_map/while
  217.5 6.5 %copy-start.2 = (bf16[1,1,96,256]{3,2,1,0:T(8,128)(2,1)S(1)}, bf16[1,1,96,256]{3,2,1,0:T(8,128)(2,1)}, u32[]{:S(2)}) copy-start(bf16[1,1,96,256]{3,2,1,0:T(8,128)(2,1)} %get-tuple-element.854) | copy-start | bytes 147460 | tf_op jit(solution)/shard_map/while
  218.2 10.0 %copy-start.7 = (bf16[1,1,96,256]{3,2,1,0:T(8,128)(2,1)S(1)}, bf16[1,1,96,256]{3,2,1,0:T(8,128)(2,1)}, u32[]{:S(2)}) copy-start(bf16[1,1,96,256]{3,2,1,0:T(8,128)(2,1)} %get-tuple-element.857) | copy-start | bytes 147460 | tf_op jit(solution)/shard_map/while
  218.5 9.7 %copy-start.31 = (pred[256]{0:T(512)(128)(4,1)S(1)}, pred[256]{0:T(512)(128)(4,1)}, u32[]{:S(2)}) copy-start(pred[256]{0:T(512)(128)(4,1)} %copy-done.30) | copy-start | bytes 772 | tf_op jit(solution)/shard_map/while
  218.5 10.1 %copy-start.28 = (pred[256]{0:T(512)(128)(4,1)S(1)}, pred[256]{0:T(512)(128)(4,1)}, u32[]{:S(2)}) copy-start(pred[256]{0:T(512)(128)(4,1)} %copy-done.27) | copy-start | bytes 772 | tf_op jit(solution)/shard_map/while
  219.4 12.5 %all-to-all-start = ((bf16[96,16,16]{0,2,1:T(8,128)(2,1)}), bf16[96,16,16]{0,2,1:T(8,128)(2,1)S(1)}, u32[]{:S(2)}, u32[]{:S(2)}) async-start(bf16[96,16,16]{0,2,1:T(8,128)(2,1)} %convert_element_type.430), calls=%async_computation | async-start | bytes 131072 | tf_op jit(solution)/shard_map/while/body/eval_jaxpr/all_to_all | solution.py:87
  230.9 19.6 %copy-start.22 = (f32[96]{0:T(128)S(1)}, f32[96]{0:T(128)}, u32[]{:S(2)}) copy-start(f32[96]{0:T(128)} %mul.953) | copy-start | bytes 1156 | tf_op jit(solution)/shard_map/while
  253.8 6.5 %copy-start.6 = (bf16[1,1,96,256]{3,2,1,0:T(8,128)(2,1)S(1)}, bf16[1,1,96,256]{3,2,1,0:T(8,128)(2,1)}, u32[]{:S(2)}) copy-start(bf16[1,1,96,256]{3,2,1,0:T(8,128)(2,1)} %get-tuple-element.856) | copy-start | bytes 147460 | tf_op jit(solution)/shard_map/while
  255.7 14.7 %all-to-all-start.1 = ((bf16[96,16,16]{0,2,1:T(8,128)(2,1)}), bf16[96,16,16]{0,2,1:T(8,128)(2,1)S(1)}, u32[]{:S(2)}, u32[]{:S(2)}) async-start(bf16[96,16,16]{0,2,1:T(8,128)(2,1)} %convert_element_type.431), calls=%async_computation.1 | async-start | bytes 131072 | tf_op jit(solution)/shard_map/while/body/eval_jaxpr/all_to_all | solution.py:87
  270.4 7.6 %copy-start.4 = (f32[2,96,432]{1,2,0:T(8,128)}, f32[2,96,432]{1,2,0:T(8,128)S(1)}, u32[]{:S(2)}) copy-start(f32[2,96,432]{1,2,0:T(8,128)S(1)} %fusion.378) | copy-start | bytes 995332 | tf_op jit(solution)/shard_map/while
  272.1 6.0 %collective-permute-start = (bf16[1536,16]{0,1:T(8,128)(2,1)S(1)}, bf16[1536,16]{0,1:T(8,128)(2,1)S(1)}, u32[]{:S(2)}, u32[]{:S(2)}) collective-permute-start(bf16[1536,16]{0,1:T(8,128)(2,1)S(1)} %get-tuple-element.790), channel_id=1, source_target_pairs={{128,0},{256,128},{384,256},{129,1},{257,129},{385,257},{130,2},{2... | collective-permute-start | bytes 147464 | tf_op jit(solution)/shard_map/while/body/eval_jaxpr/ppermute | solution.py:14
  278.1 29.5 %copy-start.30 = (pred[256]{0:T(512)(128)(4,1)}, pred[256]{0:T(512)(128)(4,1)S(1)}, u32[]{:S(2)}) copy-start(pred[256]{0:T(512)(128)(4,1)S(1)} %compare_and_fusion.7) | copy-start | bytes 772 | tf_op jit(solution)/shard_map/while
  278.1 29.5 %copy-start.27 = (pred[256]{0:T(512)(128)(4,1)}, pred[256]{0:T(512)(128)(4,1)S(1)}, u32[]{:S(2)}) copy-start(pred[256]{0:T(512)(128)(4,1)S(1)} %compare_and_fusion.8) | copy-start | bytes 772 | tf_op jit(solution)/shard_map/while
  306.9 6.5 %copy-start.2 = (bf16[1,1,96,256]{3,2,1,0:T(8,128)(2,1)S(1)}, bf16[1,1,96,256]{3,2,1,0:T(8,128)(2,1)}, u32[]{:S(2)}) copy-start(bf16[1,1,96,256]{3,2,1,0:T(8,128)(2,1)} %get-tuple-element.854) | copy-start | bytes 147460 | tf_op jit(solution)/shard_map/while
  307.6 10.0 %copy-start.7 = (bf16[1,1,96,256]{3,2,1,0:T(8,128)(2,1)S(1)}, bf16[1,1,96,256]{3,2,1,0:T(8,128)(2,1)}, u32[]{:S(2)}) copy-start(bf16[1,1,96,256]{3,2,1,0:T(8,128)(2,1)} %get-tuple-element.857) | copy-start | bytes 147460 | tf_op jit(solution)/shard_map/while
  307.9 9.7 %copy-start.31 = (pred[256]{0:T(512)(128)(4,1)S(1)}, pred[256]{0:T(512)(128)(4,1)}, u32[]{:S(2)}) copy-start(pred[256]{0:T(512)(128)(4,1)} %copy-done.30) | copy-start | bytes 772 | tf_op jit(solution)/shard_map/while
  307.9 10.1 %copy-start.28 = (pred[256]{0:T(512)(128)(4,1)S(1)}, pred[256]{0:T(512)(128)(4,1)}, u32[]{:S(2)}) copy-start(pred[256]{0:T(512)(128)(4,1)} %copy-done.27) | copy-start | bytes 772 | tf_op jit(solution)/shard_map/while
  308.8 12.5 %all-to-all-start = ((bf16[96,16,16]{0,2,1:T(8,128)(2,1)}), bf16[96,16,16]{0,2,1:T(8,128)(2,1)S(1)}, u32[]{:S(2)}, u32[]{:S(2)}) async-start(bf16[96,16,16]{0,2,1:T(8,128)(2,1)} %convert_element_type.430), calls=%async_computation | async-start | bytes 131072 | tf_op jit(solution)/shard_map/while/body/eval_jaxpr/all_to_all | solution.py:87
  320.3 19.6 %copy-start.22 = (f32[96]{0:T(128)S(1)}, f32[96]{0:T(128)}, u32[]{:S(2)}) copy-start(f32[96]{0:T(128)} %mul.953) | copy-start | bytes 1156 | tf_op jit(solution)/shard_map/while
  343.3 6.5 %copy-start.6 = (bf16[1,1,96,256]{3,2,1,0:T(8,128)(2,1)S(1)}, bf16[1,1,96,256]{3,2,1,0:T(8,128)(2,1)}, u32[]{:S(2)}) copy-start(bf16[1,1,96,256]{3,2,1,0:T(8,128)(2,1)} %get-tuple-element.856) | copy-start | bytes 147460 | tf_op jit(solution)/shard_map/while
  345.1 14.7 %all-to-all-start.1 = ((bf16[96,16,16]{0,2,1:T(8,128)(2,1)}), bf16[96,16,16]{0,2,1:T(8,128)(2,1)S(1)}, u32[]{:S(2)}, u32[]{:S(2)}) async-start(bf16[96,16,16]{0,2,1:T(8,128)(2,1)} %convert_element_type.431), calls=%async_computation.1 | async-start | bytes 131072 | tf_op jit(solution)/shard_map/while/body/eval_jaxpr/all_to_all | solution.py:87
  359.8 7.6 %copy-start.4 = (f32[2,96,432]{1,2,0:T(8,128)}, f32[2,96,432]{1,2,0:T(8,128)S(1)}, u32[]{:S(2)}) copy-start(f32[2,96,432]{1,2,0:T(8,128)S(1)} %fusion.378) | copy-start | bytes 995332 | tf_op jit(solution)/shard_map/while
  361.5 6.0 %collective-permute-start = (bf16[1536,16]{0,1:T(8,128)(2,1)S(1)}, bf16[1536,16]{0,1:T(8,128)(2,1)S(1)}, u32[]{:S(2)}, u32[]{:S(2)}) collective-permute-start(bf16[1536,16]{0,1:T(8,128)(2,1)S(1)} %get-tuple-element.790), channel_id=1, source_target_pairs={{128,0},{256,128},{384,256},{129,1},{257,129},{385,257},{130,2},{2... | collective-permute-start | bytes 147464 | tf_op jit(solution)/shard_map/while/body/eval_jaxpr/ppermute | solution.py:14
  (85 other events, 262.7 us)
Sparse Core Ops, SparseCore 0:
  370.0 89.2 all-reduce.21
where the time goes:
time: 472 us; the launch traced here: 469 us
  blocking collectives  175 us (37%)
  waiting for transfers between devices  77.5 us (16%)
  matrix products  66.1 us (14%)
  local copies, waits for them, and re-layouts  56 us (12%)
  starting transfers between devices  52.6 us (11%)
  other arithmetic  25.2 us (5%)
  between operations  14.1 us (3%)
    all_gather x8, blocking collectives, block_sharded(): grad_piece = lax.all_gather(grad_slab, 'chan', axis=1, tiled=True)  152 us
    psum x1, waiting for transfers between devices, per_device(): lax.psum((final[2], final[3], final[4], final[5]), 'dp')  65.7 us
    dot_general x72, matrix products, conv_backward(): jnp.einsum('gop,gjp->goj', grad_pre, source, preferred_element_type=jnp.f...  36.9 us
    all_to_all x8, starting transfers between devices, block_sharded(): lax.all_to_all(branch, 'chan', split_axis=1, concat_axis=0, tiled=True)  36.9 us
    psum x1, blocking collectives, per_device(): lax.psum((final[2], final[3], final[4], final[5]), 'dp')  23.8 us
    dot_general x8, matrix products, block_sharded(): fresh = jnp.dot(w_proj, grad_piece, preferred_element_type=jnp.float32)  16 us
    ppermute x4, starting transfers between devices, passed_along(): return lax.ppermute(block, axis, route)  15.7 us
    dot_general x72, matrix products, conv_backward(): jnp.einsum('goj,gop->gjp', taps_w[:, :, tap_at, :], grad_pre, preferred_e...  10.6 us
  transfers between devices with their start and end apart: 13, of which 9 were waited for; matrix products, arithmetic and copies ran while one was open for 13% of the time, Pallas kernels for 0%

commit v1 on v0

--- a/solution.py
+++ b/solution.py
@@ -78,7 +78,12 @@
 def block_sharded(grad_slab, saved_in, saved_pre, w_proj, w_conv, gain_vec, bias_vec):
     norm_state = norm_forward(saved_pre, gain_vec, bias_vec)
     act_bf = norm_state[5]
-    grad_piece = lax.all_gather(grad_slab, "chan", axis=1, tiled=True)
+    ring = [grad_slab]
+    for hop in range(15):
+        ring.append(lax.ppermute(ring[-1], "chan", [(dev, (dev + 1) % 16) for dev in range(16)]))
+    grad_piece = jnp.roll(
+        jnp.concatenate(ring[::-1], axis=1), (lax.axis_index("chan") + 1) * ring[0].shape[1], axis=1
+    )
     fresh = jnp.dot(w_proj, grad_piece, preferred_element_type=jnp.float32)
     weight_acc = lax.dot_general(
         act_bf, grad_piece, (((1,), (1,)), ((), ())), preferred_element_type=jnp.float32

time: 472 us -> 897 us (1.90)
  waiting for transfers between devices: 77.5 us -> 656 us
  blocking collectives: 175 us -> 23.8 us
  other arithmetic: 25.2 us -> 13.1 us
    ppermute x0 -> x120, waiting for transfers between devices: none -> 528 us  [block_sharded(): lax.ppermute(ring[-1], 'chan', [(dev, (dev + 1) % 16) for dev in range(16)])]
    all_gather x8 -> x0, blocking collectives: 152 us -> none  [block_sharded(): grad_piece = lax.all_gather(grad_slab, 'chan', axis=1, tiled=True)]
    all_to_all x8, waiting for transfers between devices: 4.02 us -> 59.3 us  [block_sharded(): lax.all_to_all(branch, 'chan', split_axis=1, concat_axis=0, tiled=True)]
    while x232 -> x552, local copies, waits for them, and re-layouts: 4.38 us -> 20.8 us
    dot_general x8, matrix products: 2.62 us -> 12.5 us  [block_sharded(): lax.dot_general(act_bf, grad_piece, (((1,), (1,)), ((), ())), preferred_e...]
  transfers between devices with their start and end apart: 13 -> 133, of which waited for: 9 -> 133; matrix products, arithmetic and copies ran while one was open for 13% -> 5% of each run, Pallas kernels for 0% -> 0%
where the time goes in v1:
time: 897 us; the launch traced here: 894 us
  waiting for transfers between devices  656 us (73%)
  matrix products  69.7 us (8%)
  local copies, waits for them, and re-layouts  63.1 us (7%)
  starting transfers between devices  50 us (6%)
  blocking collectives  23.8 us (3%)
  between operations  14.1 us (2%)
  other arithmetic  13.1 us (1%)
    ppermute x120, waiting for transfers between devices, block_sharded(): lax.ppermute(ring[-1], 'chan', [(dev, (dev + 1) % 16) for dev in range(16)])  528 us
    psum x1, waiting for transfers between devices, per_device(): lax.psum((final[2], final[3], final[4], final[5]), 'dp')  61 us
    all_to_all x8, waiting for transfers between devices, block_sharded(): lax.all_to_all(branch, 'chan', split_axis=1, concat_axis=0, tiled=True)  59.3 us
    dot_general x72, matrix products, conv_backward(): jnp.einsum('gop,gjp->goj', grad_pre, source, preferred_element_type=jnp.f...  36.5 us
    all_to_all x8, starting transfers between devices, block_sharded(): lax.all_to_all(branch, 'chan', split_axis=1, concat_axis=0, tiled=True)  32.1 us
    psum x1, blocking collectives, per_device(): lax.psum((final[2], final[3], final[4], final[5]), 'dp')  23.8 us
    while x552, local copies, waits for them, and re-layouts  20.8 us
  transfers between devices with their start and end apart: 133, of which 133 were waited for; matrix products, arithmetic and copies ran while one was open for 5% of the time, Pallas kernels for 0%

profile of v1, /device:TPU:2, one launch (start us, length us, event | category | flops | bytes accessed | tf_op | source)
XLA Modules:
  0.0 894.1 jit_solution(14802116649912672390)
XLA Ops:
  9.6 788.5 %while.26 = (s32[]{:T(128)}, bf16[1536,16]{0,1:T(8,128)(2,1)S(1)}, bf16[1,1,1536,16]{2,3,1,0:T(8,128)(2,1)}, f32[2,96,1536]{2,1,0:T(8,128)S(1)}, f32[2,96,432]{1...) while((s32[]{:T(128)}, bf16[1536,16]{0,1:T(8,128)(2,1)S(1)}, ...), condition=%wide.region_21.23_spmd.clone, body=%wide.region_0.22_spmd.clone.sunk | while | flops 399012256 | bytes 46313544 | solution.py:163
  10.5 4.7 collective-permute-done
  15.2 4.7 collective-permute-done.1
  19.9 4.7 collective-permute-done.2
  24.6 4.7 collective-permute-done.3
  53.0 4.7 collective-permute-done.9
  67.2 4.7 collective-permute-done.12
  71.9 4.7 collective-permute-done.13
  85.7 7.3 all-to-all-start
  93.1 7.7 all-to-all-done
  143.8 4.6 collective-permute-done.24
  162.8 4.6 collective-permute-done.28
  196.2 7.2 all-to-all-done.1
  210.5 4.7 collective-permute-done
  215.2 4.7 collective-permute-done.1
  219.9 4.7 collective-permute-done.2
  224.7 4.7 collective-permute-done.3
  253.0 4.7 collective-permute-done.9
  267.2 4.7 collective-permute-done.12
  271.9 4.7 collective-permute-done.13
  289.4 7.6 all-to-all-done
  340.0 4.6 collective-permute-done.24
  359.0 4.6 collective-permute-done.28
  392.4 7.2 all-to-all-done.1
  406.7 4.7 collective-permute-done
  411.4 4.7 collective-permute-done.1
  416.1 4.7 collective-permute-done.2
  420.8 4.7 collective-permute-done.3
  449.2 4.7 collective-permute-done.9
  463.4 4.7 collective-permute-done.12
  468.1 4.7 collective-permute-done.13
  485.6 7.6 all-to-all-done
  536.2 4.6 collective-permute-done.24
  555.2 4.6 collective-permute-done.28
  588.6 7.2 all-to-all-done.1
  602.9 4.7 collective-permute-done
  607.6 4.7 collective-permute-done.1
  612.3 4.7 collective-permute-done.2
  617.0 4.7 collective-permute-done.3
  645.4 4.7 collective-permute-done.9
  659.6 4.7 collective-permute-done.12
  664.3 4.7 collective-permute-done.13
  681.8 7.6 all-to-all-done
  732.4 4.6 collective-permute-done.24
  751.3 4.6 collective-permute-done.28
  784.8 7.2 all-to-all-done.1
  799.3 23.8 %all-reduce.18 = (f32[1,2,96]{2,1,0:T(2,128)}, f32[1,2,96]{2,1,0:T(2,128)}) all-reduce(f32[1,2,96]{2,1,0:T(2,128)S(1)} %bitcast.574, f32[1,2,96]{2,1,0:T(2,128)S(1)} %bitcast.575), channel_id=1, replica_groups=mesh['segment'=4,'chan'=16,'dp'=8] {'dp'}, use_global_device_ids=true, to_apply=%region_24.26 | all-reduce | flops 384 | bytes 3072 | tf_op jit(solution)/shard_map/psum | solution.py:165
  823.1 61.0 %all-reduce.22.cloned.1.call-done = (f32[1,2,96,1536]{3,2,1,0:T(8,128)}, f32[1,2,96,432]{3,2,1,0:T(8,128)}) async-done(((f32[1,2,96,1536]{3,2,1,0:T(8,128)}, f32[1,2,96,432]{3,2,1,0:T(8,128)}), (f32[1,2,96,1536]{3,2,1,0:T(8,128)}, f32[1,2,96,432]{3,2,1,0:T(8,128)})) %all-reduce.22.cloned.1.call-update) | async-done | bytes 1511440 | tf_op jit(solution)/shard_map/psum | solution.py:165
  (1243 shorter events, 555.3 us)
Async XLA Ops:
  7.2 876.9 %all-reduce.22.cloned.1.call-start = ((), (), s32[]{:S(2)}) async-start(), calls=%async_computation.2 | async-start | bytes 3145728 | tf_op jit(solution)/shard_map/psum | solution.py:165
  19.9 4.7 collective-permute-start.2
  24.6 4.7 collective-permute-start.3
  43.5 4.7 collective-permute-start.7
  48.3 4.7 collective-permute-start.8
  67.2 4.7 collective-permute-start.12
  71.9 4.7 collective-permute-start.13
  85.7 15.2 %all-to-all-start = ((bf16[96,16,16]{0,2,1:T(8,128)(2,1)}), bf16[96,16,16]{0,2,1:T(8,128)(2,1)S(1)}, u32[]{:S(2)}, u32[]{:S(2)}) async-start(bf16[96,16,16]{0,2,1:T(8,128)(2,1)} %convert_element_type.430), calls=%async_computation | async-start | bytes 131072 | tf_op jit(solution)/shard_map/while/body/eval_jaxpr/all_to_all | solution.py:92
  101.1 4.7 collective-permute-start.15
  110.6 4.7 collective-permute-start.17
  115.3 4.7 collective-permute-start.18
  134.2 4.7 collective-permute-start.22
  138.9 4.7 collective-permute-start.23
  143.7 4.7 collective-permute-start.24
  148.4 4.7 collective-permute-start.25
  153.1 4.7 collective-permute-start.26
  157.8 4.7 collective-permute-start.27
  162.6 4.8 collective-permute-start.28
  167.5 5.1 collective-permute-start.29
  192.1 11.3 %all-to-all-start.1 = ((bf16[96,16,16]{0,2,1:T(8,128)(2,1)}), bf16[96,16,16]{0,2,1:T(8,128)(2,1)S(1)}, u32[]{:S(2)}, u32[]{:S(2)}) async-start(bf16[96,16,16]{0,2,1:T(8,128)(2,1)} %convert_element_type.431), calls=%async_computation.1 | async-start | bytes 131072 | tf_op jit(solution)/shard_map/while/body/eval_jaxpr/all_to_all | solution.py:92
  203.6 6.0 collective-permute-start.30
  219.9 4.7 collective-permute-start.2
  224.7 4.7 collective-permute-start.3
  238.8 4.7 collective-permute-start.6
  243.6 4.7 collective-permute-start.7
  248.3 4.7 collective-permute-start.8
  262.5 4.7 collective-permute-start.11
  267.2 4.7 collective-permute-start.12
  285.7 11.4 %all-to-all-start = ((bf16[96,16,16]{0,2,1:T(8,128)(2,1)}), bf16[96,16,16]{0,2,1:T(8,128)(2,1)S(1)}, u32[]{:S(2)}, u32[]{:S(2)}) async-start(bf16[96,16,16]{0,2,1:T(8,128)(2,1)} %convert_element_type.430), calls=%async_computation | async-start | bytes 131072 | tf_op jit(solution)/shard_map/while/body/eval_jaxpr/all_to_all | solution.py:92
  297.3 4.7 collective-permute-start.15
  311.5 4.7 collective-permute-start.18
  316.2 4.7 collective-permute-start.19
  358.8 4.8 collective-permute-start.28
  363.7 5.1 collective-permute-start.29
  388.3 11.3 %all-to-all-start.1 = ((bf16[96,16,16]{0,2,1:T(8,128)(2,1)}), bf16[96,16,16]{0,2,1:T(8,128)(2,1)S(1)}, u32[]{:S(2)}, u32[]{:S(2)}) async-start(bf16[96,16,16]{0,2,1:T(8,128)(2,1)} %convert_element_type.431), calls=%async_computation.1 | async-start | bytes 131072 | tf_op jit(solution)/shard_map/while/body/eval_jaxpr/all_to_all | solution.py:92
  399.8 6.0 collective-permute-start.30
  481.9 11.4 %all-to-all-start = ((bf16[96,16,16]{0,2,1:T(8,128)(2,1)}), bf16[96,16,16]{0,2,1:T(8,128)(2,1)S(1)}, u32[]{:S(2)}, u32[]{:S(2)}) async-start(bf16[96,16,16]{0,2,1:T(8,128)(2,1)} %convert_element_type.430), calls=%async_computation | async-start | bytes 131072 | tf_op jit(solution)/shard_map/while/body/eval_jaxpr/all_to_all | solution.py:92
  493.5 4.7 collective-permute-start.15
  555.0 4.8 collective-permute-start.28
  559.9 5.1 collective-permute-start.29
  584.5 11.3 %all-to-all-start.1 = ((bf16[96,16,16]{0,2,1:T(8,128)(2,1)}), bf16[96,16,16]{0,2,1:T(8,128)(2,1)S(1)}, u32[]{:S(2)}, u32[]{:S(2)}) async-start(bf16[96,16,16]{0,2,1:T(8,128)(2,1)} %convert_element_type.431), calls=%async_computation.1 | async-start | bytes 131072 | tf_op jit(solution)/shard_map/while/body/eval_jaxpr/all_to_all | solution.py:92
  596.0 6.0 collective-permute-start.30
  678.1 11.4 %all-to-all-start = ((bf16[96,16,16]{0,2,1:T(8,128)(2,1)}), bf16[96,16,16]{0,2,1:T(8,128)(2,1)S(1)}, u32[]{:S(2)}, u32[]{:S(2)}) async-start(bf16[96,16,16]{0,2,1:T(8,128)(2,1)} %convert_element_type.430), calls=%async_computation | async-start | bytes 131072 | tf_op jit(solution)/shard_map/while/body/eval_jaxpr/all_to_all | solution.py:92
  689.7 4.7 collective-permute-start.15
  751.1 4.8 collective-permute-start.28
  756.0 5.1 collective-permute-start.29
  780.6 11.3 %all-to-all-start.1 = ((bf16[96,16,16]{0,2,1:T(8,128)(2,1)}), bf16[96,16,16]{0,2,1:T(8,128)(2,1)S(1)}, u32[]{:S(2)}, u32[]{:S(2)}) async-start(bf16[96,16,16]{0,2,1:T(8,128)(2,1)} %convert_element_type.431), calls=%async_computation.1 | async-start | bytes 131072 | tf_op jit(solution)/shard_map/while/body/eval_jaxpr/all_to_all | solution.py:92
  792.1 6.0 collective-permute-start.30
  (305 other events, 4008.8 us)
Sparse Core Ops, SparseCore 0:
  799.5 84.6 all-reduce.21
